TPU v7x, 32 devices: a whole 2x2x4 slice. The times are simulated.
32 devices in a mesh: gx: 4 (over x, core), gy: 4 (over z), gz: 2 (over y).
Axes of the slice: x: 2, y: 2, z: 4, core: 2. Of those that a mesh axis runs over, the one named last changes fastest.
Arguments:
- positions: float32 [3, 16384], P(None, ('gx', 'gy', 'gz')), may hold values from 0 to 4, as said below
- velocities: float32 [3, 16384], P(None, ('gx', 'gy', 'gz')), may hold values from -3 to 3
- star_mass: float32 [16384], P(('gx', 'gy', 'gz')), may hold values from 0.0009765625 to 0.00390625
- far_previous: float32 [3, 16384], P(None, ('gx', 'gy', 'gz')), may hold values from -6 to 6
- cell_index: int32 [16384], P(('gx', 'gy', 'gz')), may hold values from 0 to 15, as said below
- ghost_list: int32 [8192], P(('gx', 'gy', 'gz')), may hold values from 0 to 511, as said below
- block_index: int32 [512, 128], P(('gx', 'gy', 'gz')), may hold values from 0 to 7423, as said below
- block_owner: int32 [512, 1], P(('gx', 'gy', 'gz')), may hold values from 0 to 1; in each aligned block of 16 rows (0 to 15, 16 to 31, ...) at most 16 rows name the same one
- substeps: int32 [512], P(('gx', 'gy', 'gz')), may hold values from 1 to 8, as said below
Outputs:
- far_acc: float32 [3, 16384], P(None, ('gx', 'gy', 'gz'))
- block_state: float32 [6, 131072], P(None, ('gx', 'gy', 'gz'))
Inputs may be any that keep to these rules, and one draw needn't show every extreme that they name: `positions`: stars of the domain with coordinates (a, b, c) lie inside the unit box whose lowest corner is (a, b, c). `cell_index`: each cell of a domain is a box of a regular split of the domain's box, and holds at least 16 of its stars. `ghost_list`: A domain's 256 entries are distinct. `block_index`: each block's 128 entries are distinct pool columns of stars around one of the domain's own stars; no entry is a column of the domain's own sent stars or of a domain outside the grid. `block_owner`: no more than 16 of one domain's blocks have the same owner; in every draw some domain gives exactly 16 blocks to one owner. Every domain has a block with 8 substeps.
All inputs are finite; a program needn't handle non-finite values.
Results may differ from a plain program's by a relative error of at most 0.0003.
Values sent between devices are 32-bit elements; how exact they have to be, the bound alone decides.
A program may use at most 64 MiB of HBM per device.

v0:
```python
import math

import jax
import jax.numpy as jnp
from jax import lax
from jax.sharding import PartitionSpec as P

CELLS = 16
BLOCKS_DEV = 16
SUBMAX = 8


SOFTENING = 0.0025
INNER_RADIUS = 0.25
OUTER_RADIUS = 1.0
TIME_STEP = 0.25


def padded(cells, sides, width):
    for axis, dim in sides:
        count = lax.axis_size(axis)
        ends = count - 1
        head = lax.slice_in_dim(cells, 0, width, axis=dim)
        tail = lax.slice_in_dim(cells, cells.shape[dim] - width, cells.shape[dim], axis=dim)
        cells = jnp.concatenate(
            [
                lax.ppermute(tail, axis, [(i, (i + 1) % count) for i in range(ends)]),
                cells,
                lax.ppermute(head, axis, [((i + 1) % count, i) for i in range(ends)]),
            ],
            axis=dim,
        )
    return cells


def changeover(radius):
    fraction = jnp.clip((radius - INNER_RADIUS) / (OUTER_RADIUS - INNER_RADIUS), 0.0, 1.0)
    return 1.0 - fraction * fraction * (3.0 - 2.0 * fraction)


def evaluate(position, velocity, masses):
    offset = position[:, :, None, :] - position[:, :, :, None]
    relative = velocity[:, :, None, :] - velocity[:, :, :, None]
    square = jnp.sum(offset * offset, axis=0) + SOFTENING
    radius = jnp.sqrt(square)
    weight = masses[:, None, :] * changeover(radius) / (square * radius)
    radial_rate = jnp.sum(offset * relative, axis=0) / square
    acceleration = jnp.sum(weight[None] * offset, axis=-1)
    jerk_term = jnp.sum(weight[None] * (relative - 3.0 * radial_rate[None] * offset), axis=-1)
    return (acceleration, jerk_term)


def integrate(state, step_count):
    start_position = state[0:3]
    start_velocity = state[3:6]
    position = start_position
    velocity = start_velocity
    masses = state[6]
    widths = (TIME_STEP / jnp.maximum(step_count, 1.0))[None, :, None]
    squared = widths * widths
    acc_old, jerk_old = evaluate(position, velocity, masses)
    for number in range(SUBMAX):
        live = (step_count > number)[None, :, None]
        predicted = (
            position
            + widths * velocity
            + 0.5 * squared * acc_old
            + squared * widths / 6.0 * jerk_old
        )
        predicted_vel = velocity + widths * acc_old + 0.5 * squared * jerk_old
        acc_new, jerk_new = evaluate(predicted, predicted_vel, masses)
        velocity_new = (
            velocity + 0.5 * widths * (acc_old + acc_new) + squared / 12.0 * (jerk_old - jerk_new)
        )
        position_new = (
            position
            + 0.5 * widths * (velocity + velocity_new)
            + squared / 12.0 * (acc_old - acc_new)
        )
        position = jnp.where(live, position_new, position)
        velocity = jnp.where(live, velocity_new, velocity)
        acc_old = jnp.where(live, acc_new, acc_old)
        jerk_old = jnp.where(live, jerk_new, jerk_old)
    return jnp.concatenate([position - start_position, velocity - start_velocity], axis=0)


def grouped(state, step_count):
    total = state.shape[1]
    group = math.gcd(total, 4)
    rows = state.shape[0]
    split = state.reshape(rows, total // group, group, state.shape[2]).transpose(1, 0, 2, 3)
    counts = step_count.reshape(total // group, group)
    done = lax.map(lambda inputs: integrate(inputs[0], inputs[1]), (split, counts))
    return done.transpose(1, 0, 2, 3).reshape(6, total, state.shape[2])


def far_block(total, cells, stars):
    offset = cells[1:4, :, None] - stars[:, None, :]
    square = jnp.sum(offset * offset, axis=0) + SOFTENING
    radius = jnp.sqrt(square)
    weight = cells[0][:, None] * (1.0 - changeover(radius)) / (square * radius)
    return total + jnp.sum(weight[None] * offset, axis=1)


def far_field(stars, cells):
    width = math.gcd(cells.shape[1], 512)
    blocks = cells.reshape(4, cells.shape[1] // width, width).transpose(1, 0, 2)

    def step(carry, piece):
        return (far_block(carry, piece, stars), None)

    total, unused = lax.scan(step, jnp.zeros_like(stars), blocks)
    return total


def on_device(
    positions,
    velocities,
    star_mass,
    far_previous,
    cell_index,
    ghost_list,
    block_index,
    block_owner,
    substeps,
):
    lanes = lax.axis_size("gz")
    capacity = max(2, 2 * BLOCKS_DEV // lanes)
    block_len = block_index.shape[1]
    ghost_count = ghost_list.shape[0]
    membership = (cell_index[None, :] == jnp.arange(CELLS, dtype=jnp.int32)[:, None]).astype(
        jnp.float32
    )
    cell_mass = jnp.dot(membership, star_mass, precision=lax.Precision.HIGHEST)
    weighted = jnp.dot(positions * star_mass[None], membership.T, precision=lax.Precision.HIGHEST)
    moments = jnp.concatenate([cell_mass[None], weighted / cell_mass[None]], axis=0)
    far_acc = far_field(positions, lax.all_gather(moments, ("gx", "gy", "gz"), axis=1, tiled=True))
    kicked = velocities + far_previous * (0.5 * TIME_STEP)
    local_rows = jnp.concatenate([positions, kicked, star_mass[None]], axis=0)
    ghost_rows = local_rows[:, ghost_list].reshape(7, 1, 1, 1, ghost_count)
    near = padded(ghost_rows, (("gx", 1), ("gy", 2), ("gz", 3)), 1)
    pool = jnp.concatenate([local_rows, near.reshape(7, 27 * ghost_count)], axis=1)
    gathered = pool[:, block_index]
    step_count = substeps.astype(jnp.float32)
    owners = block_owner[:, 0]
    marks = (owners[:, None] == jnp.arange(lanes, dtype=jnp.int32)[None, :]).astype(jnp.int32)
    ranks = jnp.sum((jnp.cumsum(marks, axis=0) - marks) * marks, axis=1)
    slots = owners * capacity + ranks
    placing = (slots[None, :] == jnp.arange(lanes * capacity, dtype=jnp.int32)[:, None]).astype(
        jnp.float32
    )
    results = grouped(gathered, step_count)
    packed = jnp.einsum("ns,rst->rnt", placing, results, precision=lax.Precision.HIGHEST)
    packed = packed.reshape(6, lanes, capacity, block_len)
    arrived = lax.all_to_all(packed, "gz", split_axis=1, concat_axis=1, tiled=True)
    return (far_acc, arrived.reshape(6, lanes * capacity * block_len))


def solution(mesh):
    placed = (
        P(None, ("gx", "gy", "gz")),
        P(None, ("gx", "gy", "gz")),
        P(("gx", "gy", "gz")),
        P(None, ("gx", "gy", "gz")),
        P(("gx", "gy", "gz")),
        P(("gx", "gy", "gz")),
        P(("gx", "gy", "gz"), None),
        P(("gx", "gy", "gz"), None),
        P(("gx", "gy", "gz")),
    )
    return jax.shard_map(
        on_device,
        mesh=mesh,
        in_specs=placed,
        out_specs=(P(None, ("gx", "gy", "gz")), P(None, ("gx", "gy", "gz"))),
        check_vma=False,
    )
```

profile of v0, /device:TPU:0, one launch (start us, length us, event | category | flops | bytes accessed | tf_op | source)
XLA Modules:
  0.0 182.7 jit_solution(13769333240568929299)
XLA Ops:
  3.7 2.4 %collective-permute-start = (f32[7,1,1,1,256]{0,4,3,2,1:T(8,128)S(1)}, f32[7,1,1,1,256]{0,4,3,2,1:T(8,128)S(1)}, u32[]{:S(2)}, u32[]{:S(2)}) collective-permute-start(f32[7,1,1,1,256]{0,4,3,2,1:T(8,128)S(1)} %bitcast.114), channel_id=1, source_target_pairs={{0,8},{8,16},{16,24},{1,9},{9,17},{17,25},{2,10},{10,18},{18,26},{... | collective-permute-start | bytes 21512 | tf_op jit(solution)/shard_map/ppermute | solution.py:27
  6.1 1.3 collective-permute-start.1
  9.1 70.8 %all-gather = f32[32,16,4]{1,2,0:T(4,128)S(1)} all-gather(f32[1,16,4]{1,2,0:T(4,128)S(1)} %maximum_bitcast_fusion.1), channel_id=1, replica_groups=mesh['gx'=4,'gy'=4,'gz'=2] {'gx','gy','gz'}, dimensions={0}, use_global_device_ids=true | all-gather | bytes 8448 | tf_op jit(solution)/shard_map/all_gather | solution.py:137
  80.8 1.2 fusion.73
  83.1 1.3 collective-permute-start.2
  84.4 1.3 collective-permute-start.3
  85.9 4.2 %collective-permute-done.3 = f32[7,3,1,1,256]{4,3,2,1,0:T(1,128)S(1)} collective-permute-done((f32[7,3,1,1,256]{4,3,2,1,0:T(1,128)S(1)}, f32[7,3,1,1,256]{4,3,2,1,0:T(1,128)S(1)}, u32[]{:S(2)}, u32[]{:S(2)}) %collective-permute-start.3) | collective-permute-done | bytes 21536 | tf_op jit(solution)/shard_map/ppermute | solution.py:29
  90.1 1.3 collective-permute-start.4
  91.4 1.3 collective-permute-start.5
  93.3 4.3 %collective-permute-done.5 = f32[7,3,3,1,256]{4,3,2,1,0:T(1,128)S(1)} collective-permute-done((f32[7,3,3,1,256]{4,3,2,1,0:T(1,128)S(1)}, f32[7,3,3,1,256]{4,3,2,1,0:T(1,128)S(1)}, u32[]{:S(2)}, u32[]{:S(2)}) %collective-permute-start.5) | collective-permute-done | bytes 64544 | tf_op jit(solution)/shard_map/ppermute | solution.py:29
  97.7 2.5 %copy.60 = f32[7,7424]{0,1:T(8,128)} copy(f32[7,7424]{1,0:T(8,128)S(1)} %pad_maximum_fusion) | data formatting | bytes 415744 | tf_op jit(solution)/shard_map/concatenate | solution.py:142
  100.2 7.5 %gather_fusion.1 = f32[2048,7]{1,0:T(8,128)S(1)} fusion(f32[7,7424]{0,1:T(8,128)} %copy.60, s32[2048]{0:T(1024)S(1)} %fusion.82), kind=kCustom, calls=%fused_computation.1 | custom fusion | bytes 122880 | tf_op jit(solution)/shard_map/gather | solution.py:143
  108.1 65.2 %while.17 = (s32[]{:T(128)}, f32[4,6,4,128]{3,2,1,0:T(4,128)S(1)}, f32[4,4]{1,0:T(4,128)S(1)}, f32[4,7,4,128]{3,2,0,1:T(4,128)S(1)}, s32[]{:T(128)}) while((s32[]{:T(128)}, f32[4,6,4,128]{3,2,1,0:T(4,128)S(1)}, f32[4,4]{1,0:T(4,128)S(1)}, f32[4,7,4,128]{3,2,0,1:T(4,128)S(1)}, s32[]{:T(128)}) %tuple.206), condition=%wide.region_39.40_spmd, body=%wide.region_2.39_spmd.sunk | while | flops 32209984 | bytes 20266372 | solution.py:93
  109.0 1.0 fusion.112
  110.7 1.0 fusion.114
  112.6 1.0 fusion.116
  114.4 1.0 fusion.118
  116.2 1.0 fusion.120
  118.0 1.0 fusion.122
  119.8 1.0 fusion.124
  121.6 1.0 fusion.126
  123.4 1.0 fusion.128
  125.2 1.0 fusion.112
  127.0 1.0 fusion.114
  128.8 1.0 fusion.116
  130.6 1.0 fusion.118
  132.4 1.0 fusion.120
  134.3 1.0 fusion.122
  136.1 1.0 fusion.124
  137.9 1.0 fusion.126
  139.7 1.0 fusion.128
  141.5 1.0 fusion.112
  143.3 1.0 fusion.114
  145.1 1.0 fusion.116
  146.9 1.0 fusion.118
  148.7 1.0 fusion.120
  150.5 1.0 fusion.122
  152.3 1.0 fusion.124
  154.2 1.0 fusion.126
  156.0 1.0 fusion.128
  157.8 1.0 fusion.112
  159.5 1.0 fusion.114
  161.4 1.0 fusion.116
  163.2 1.0 fusion.118
  166.8 1.0 fusion.122
  174.3 3.3 %all-to-all-start = ((f32[6,2,16,128]{3,2,0,1:T(8,128)}), f32[6,2,16,128]{3,2,0,1:T(8,128)S(1)}, u32[]{:S(2)}, u32[]{:S(2)}) async-start(f32[6,2,16,128]{3,2,0,1:T(8,128)} %copy.64), calls=%async_computation | async-start | bytes 196608 | tf_op jit(solution)/shard_map/all_to_all | solution.py:155
  177.6 1.0 fusion.74
  178.6 3.3 %all-to-all-done = f32[6,2,16,128]{3,2,0,1:T(8,128)S(1)} async-done(((f32[6,2,16,128]{3,2,0,1:T(8,128)}), f32[6,2,16,128]{3,2,0,1:T(8,128)S(1)}, u32[]{:S(2)}, u32[]{:S(2)}) %all-to-all-start) | async-done | bytes 98336 | tf_op jit(solution)/shard_map/all_to_all | solution.py:155
  (222 shorter events, 43.3 us)
Async XLA Ops:
  0.6 97.0 %copy-start.1 = (f32[512]{0:T(512)S(1)}, f32[512]{0:T(512)}, u32[]{:S(2)}) copy-start(f32[512]{0:T(512)} %param.13) | copy-start | bytes 6148
  0.6 97.0 %copy-start = (f32[3,512]{1,0:T(4,128)S(1)}, f32[3,512]{1,0:T(4,128)}, u32[]{:S(2)}) copy-start(f32[3,512]{1,0:T(4,128)} %param.11) | copy-start | bytes 18436
  0.7 82.0 %copy-start.2 = (s32[16,1]{0,1:T(1,128)S(1)}, s32[16,1]{0,1:T(1,128)}, u32[]{:S(2)}) copy-start(s32[16,1]{0,1:T(1,128)} %param.18) | copy-start | bytes 196
  0.7 92.1 %copy-start.3 = (s32[16]{0:T(128)S(1)}, s32[16]{0:T(128)}, u32[]{:S(2)}) copy-start(s32[16]{0:T(128)} %param.19) | copy-start | bytes 196
  3.7 79.2 %collective-permute-start = (f32[7,1,1,1,256]{0,4,3,2,1:T(8,128)S(1)}, f32[7,1,1,1,256]{0,4,3,2,1:T(8,128)S(1)}, u32[]{:S(2)}, u32[]{:S(2)}) collective-permute-start(f32[7,1,1,1,256]{0,4,3,2,1:T(8,128)S(1)} %bitcast.114), channel_id=1, source_target_pairs={{0,8},{8,16},{16,24},{1,9},{9,17},{17,25},{2,10},{10,18},{18,26},{... | collective-permute-start | bytes 21512 | tf_op jit(solution)/shard_map/ppermute | solution.py:27
  6.1 76.8 %collective-permute-start.1 = (f32[7,1,1,1,256]{0,4,3,2,1:T(8,128)S(1)}, f32[7,1,1,1,256]{0,4,3,2,1:T(8,128)S(1)}, u32[]{:S(2)}, u32[]{:S(2)}) collective-permute-start(f32[7,1,1,1,256]{0,4,3,2,1:T(8,128)S(1)} %bitcast.115), channel_id=1, source_target_pairs={{8,0},{16,8},{24,16},{9,1},{17,9},{25,17},{10,2},{18,10},{26,18},{... | collective-permute-start | bytes 21512 | tf_op jit(solution)/shard_map/ppermute | solution.py:29
  83.1 2.8 %collective-permute-start.2 = (f32[7,3,1,1,256]{4,3,2,1,0:T(1,128)S(1)}, f32[7,3,1,1,256]{4,3,2,1,0:T(1,128)S(1)}, u32[]{:S(2)}, u32[]{:S(2)}) collective-permute-start(f32[7,3,1,1,256]{4,3,2,1,0:T(1,128)S(1)} %pad_maximum_fusion.3), channel_id=1, source_target_pairs={{0,2},{2,4},{4,6},{1,3},{3,5},{5,7},{8,10},{10,12},{12,14},{9,11},... | collective-permute-start | bytes 64520 | tf_op jit(solution)/shard_map/ppermute | solution.py:27
  84.4 5.7 %collective-permute-start.3 = (f32[7,3,1,1,256]{4,3,2,1,0:T(1,128)S(1)}, f32[7,3,1,1,256]{4,3,2,1,0:T(1,128)S(1)}, u32[]{:S(2)}, u32[]{:S(2)}) collective-permute-start(f32[7,3,1,1,256]{4,3,2,1,0:T(1,128)S(1)} %pad_maximum_fusion.3), channel_id=1, source_target_pairs={{2,0},{4,2},{6,4},{3,1},{5,3},{7,5},{10,8},{12,10},{14,12},{11,9},... | collective-permute-start | bytes 64520 | tf_op jit(solution)/shard_map/ppermute | solution.py:29
  90.1 3.2 %collective-permute-start.4 = (f32[7,3,3,1,256]{4,3,2,1,0:T(1,128)S(1)}, f32[7,3,3,1,256]{4,3,2,1,0:T(1,128)S(1)}, u32[]{:S(2)}, u32[]{:S(2)}) collective-permute-start(f32[7,3,3,1,256]{4,3,2,1,0:T(1,128)S(1)} %pad_maximum_fusion.2), channel_id=1, source_target_pairs={{0,1},{2,3},{4,5},{6,7},{8,9},{10,11},{12,13},{14,15},{16,17},{18,... | collective-permute-start | bytes 193544 | tf_op jit(solution)/shard_map/ppermute | solution.py:27
  91.4 6.1 %collective-permute-start.5 = (f32[7,3,3,1,256]{4,3,2,1,0:T(1,128)S(1)}, f32[7,3,3,1,256]{4,3,2,1,0:T(1,128)S(1)}, u32[]{:S(2)}, u32[]{:S(2)}) collective-permute-start(f32[7,3,3,1,256]{4,3,2,1,0:T(1,128)S(1)} %pad_maximum_fusion.2), channel_id=1, source_target_pairs={{1,0},{3,2},{5,4},{7,6},{9,8},{11,10},{13,12},{15,14},{17,16},{19,... | collective-permute-start | bytes 193544 | tf_op jit(solution)/shard_map/ppermute | solution.py:29
  174.3 7.6 %all-to-all-start = ((f32[6,2,16,128]{3,2,0,1:T(8,128)}), f32[6,2,16,128]{3,2,0,1:T(8,128)S(1)}, u32[]{:S(2)}, u32[]{:S(2)}) async-start(f32[6,2,16,128]{3,2,0,1:T(8,128)} %copy.64), calls=%async_computation | async-start | bytes 196608 | tf_op jit(solution)/shard_map/all_to_all | solution.py:155
where the time goes:
time: 183 us
  blocking collectives  70.8 us (39%)
  other arithmetic  70.5 us (39%)
  local copies, waits for them, and re-layouts  13.2 us (7%)
  starting transfers between devices  12.2 us (7%)
  waiting for transfers between devices  12.2 us (7%)
  matrix products  1.99 us (1%)
    all_gather x1, blocking collectives, on_device(): lax.all_gather(moments, ('gx', 'gy', 'gz'), axis=1, tiled=True)  70.8 us
    reduce_sum x36, other arithmetic, evaluate(): acceleration = jnp.sum(weight[None] * offset, axis=-1)  34.4 us
    reduce_sum x36, other arithmetic, evaluate(): square = jnp.sum(offset * offset, axis=0) + SOFTENING  17 us
    ppermute x3, waiting for transfers between devices, padded(): lax.ppermute(head, axis, [((i + 1) % count, i) for i in range(ends)])  8.46 us
    gather x2, local copies, waits for them, and re-layouts, on_device(): gathered = pool[:, block_index]  7.87 us
    mul x36, other arithmetic, evaluate(): 3.0 * radial_rate[None] * offset  7.41 us
    ppermute x3, starting transfers between devices, padded(): lax.ppermute(tail, axis, [(i, (i + 1) % count) for i in range(ends)])  4.99 us
    ppermute x3, starting transfers between devices, padded(): lax.ppermute(head, axis, [((i + 1) % count, i) for i in range(ends)])  3.88 us
  transfers between devices with their start and end apart: 7, of which 4 were waited for; matrix products, arithmetic and copies ran while one was open for 3% of the time, Pallas kernels for 0%

commit v1 on v0

v1 whole, which is shorter than its diff:
```python
import functools

import jax
import jax.numpy as jnp
from jax import lax
from jax.experimental import pallas as pl
from jax.experimental.pallas import tpu as pltpu
from jax.sharding import PartitionSpec as P

CELLS = 16
BLOCKS_DEV = 16
SUBMAX = 8
AXES = ("gx", "gy", "gz")
MESH = pl.DeviceIdType.MESH
LANES = 128

SOFTENING = 0.0025
INNER_RADIUS = 0.25
OUTER_RADIUS = 1.0
TIME_STEP = 0.25
SPAN = OUTER_RADIUS - INNER_RADIUS

BF16 = jnp.bfloat16
F32 = jnp.float32


def three(value):
    high = value.astype(BF16).astype(F32)
    rest = value - high
    middle = rest.astype(BF16).astype(F32)
    low = (rest - middle).astype(BF16).astype(F32)
    return high, middle, low


def pick(chunks, index):
    index = jnp.broadcast_to(index, (8, LANES))
    lane, chunk = index & (LANES - 1), index >> 7
    found = jnp.zeros((8, LANES), F32)
    for number, piece in chunks:
        found = jnp.where(chunk == number, jnp.take_along_axis(piece, lane, axis=1), found)
    return found


def prepare(pos_ref, vel_ref, mass_ref, far_ref, cell_ref, ghost_ref, rows_ref, sent_ref, moment_ref):
    stars = pos_ref.shape[1]
    position, mass = pos_ref[...], mass_ref[...]
    kicked = vel_ref[...] + far_ref[...] * (0.5 * TIME_STEP)
    rows = jnp.concatenate([position, kicked, mass, jnp.zeros((1, stars), F32)], axis=0)
    chunks = []
    for number in range(stars // LANES):
        piece = rows[:, number * LANES : (number + 1) * LANES]
        rows_ref[number] = piece
        chunks.append((number, piece))
    for number in range(ghost_ref.shape[1] // LANES):
        sent_ref[number] = pick(chunks, ghost_ref[:, number * LANES : (number + 1) * LANES])
    cell = lax.broadcasted_iota(jnp.int32, (LANES, stars), 0)
    member = jnp.where(jnp.broadcast_to(cell_ref[...], (LANES, stars)) == cell, 1.0, 0.0).astype(BF16)
    weighted = jnp.concatenate([mass, position * mass, jnp.zeros((4, stars), F32)], axis=0)
    parts = jnp.concatenate([*three(weighted), jnp.zeros_like(weighted)], axis=0).astype(BF16)
    sums = lax.dot_general(parts, member, (((1,), (1,)), ((), ())), preferred_element_type=F32)
    sums = sums[0:8] + sums[8:16] + sums[16:24]
    inside = lax.broadcasted_iota(jnp.int32, (1, LANES), 1) < CELLS
    total = jnp.where(inside, sums[0:1], 0.0)
    packed = total
    for axis in range(3):
        centre = jnp.where(inside, sums[axis + 1 : axis + 2] / jnp.where(inside, total, 1.0), 0.0)
        packed = packed + pltpu.roll(centre, (axis + 1) * CELLS, 1)
    moment_ref[0] = packed


def coordinates(sizes, number):
    return number // (sizes[1] * sizes[2]), number // sizes[2] % sizes[1], number % sizes[2]


def exchange(sizes, sent_ref, moment_ref, near_ref, every_ref, own_sem, moment_sems, send_sems, recv_sems):
    count = sizes[0] * sizes[1] * sizes[2]
    here = tuple(lax.axis_index(axis) for axis in AXES)
    me = (here[0] * sizes[1] + here[1]) * sizes[2] + here[2]
    barrier = pltpu.get_barrier_semaphore()

    def other(step):
        return coordinates(sizes, lax.rem(me + step, count))

    def greet(step, carry):
        pl.semaphore_signal(barrier, inc=1, device_id=other(step), device_id_type=MESH)
        return carry

    lax.fori_loop(1, count, greet, 0)
    own = pltpu.make_async_copy(moment_ref.at[0], every_ref.at[0], own_sem)
    own.start()
    pl.semaphore_wait(barrier, count - 1)

    def share(step, carry):
        pltpu.make_async_remote_copy(
            src_ref=moment_ref.at[0],
            dst_ref=every_ref.at[step],
            send_sem=moment_sems.at[0],
            recv_sem=moment_sems.at[1],
            device_id=other(step),
            device_id_type=MESH,
        ).start()
        return carry

    lax.fori_loop(1, count, share, 0)

    def around(number):
        offset = (number // 9 - 1, number // 3 % 3 - 1, number % 3 - 1)
        there = tuple(a + b for a, b in zip(here, offset))
        inside = functools.reduce(
            jnp.logical_and, [(a >= 0) & (a < size) for a, size in zip(there, sizes)]
        )
        return there, inside

    def copy(number, there):
        return pltpu.make_async_remote_copy(
            src_ref=sent_ref,
            dst_ref=near_ref.at[26 - number],
            send_sem=send_sems.at[number],
            recv_sem=recv_sems.at[26 - number],
            device_id=there,
            device_id_type=MESH,
        )

    for number in range(27):
        if number != 13:
            there, inside = around(number)

            @pl.when(inside)
            def _():
                copy(number, there).start()

    own.wait()
    rest = every_ref.at[pl.ds(1, count - 1)]
    pltpu.make_async_copy(rest, rest, moment_sems.at[0]).wait()
    pltpu.make_async_copy(rest, rest, moment_sems.at[1]).wait()
    for number in range(27):
        if number != 13:
            there, inside = around(number)

            @pl.when(inside)
            def _():
                pltpu.make_async_copy(sent_ref, sent_ref, send_sems.at[number]).wait()
                pltpu.make_async_copy(near_ref.at[number], near_ref.at[number], recv_sems.at[number]).wait()


def forces(position, velocity, mass):
    norm = jnp.sum(position * position, axis=0, keepdims=True) + 0.5 * SOFTENING
    mixed = jnp.sum(position * velocity, axis=0, keepdims=True)
    one = jnp.ones_like(norm)
    nought = jnp.zeros_like(norm)
    nought3 = jnp.zeros_like(position)
    left = jnp.concatenate([position, velocity, norm, mixed], axis=0)
    left_h, left_m, left_l = three(left)
    ones8 = jnp.ones_like(left)
    zeros8 = jnp.zeros_like(left)
    left_all = jnp.concatenate([left_h, left_h, left_h, left_m, left_m, left_l, ones8, zeros8], axis=0)

    pos_parts = three(position)
    vel_parts = three(velocity)
    norm_parts = three(norm)
    mixed_parts = three(mixed)

    def right(kind):
        if kind == 0:
            groups = [
                jnp.concatenate([-2.0 * part, nought3, one if k == 0 else nought, nought], axis=0)
                for k, part in enumerate(pos_parts)
            ]
            last = jnp.concatenate([*norm_parts, nought3, nought, nought], axis=0)
        else:
            groups = [
                jnp.concatenate([-v, -p, nought, one if k == 0 else nought], axis=0)
                for k, (p, v) in enumerate(zip(pos_parts, vel_parts))
            ]
            last = jnp.concatenate([*mixed_parts, nought3, nought, nought], axis=0)
        first, second, third = groups
        return jnp.concatenate([first, second, third, first, second, first, last, zeros8], axis=0)

    right_all = jnp.concatenate([right(0), right(1)], axis=1)
    pairs = lax.dot_general(
        left_all.astype(BF16),
        right_all.astype(BF16),
        (((0,), (0,)), ((), ())),
        preferred_element_type=F32,
    )
    square, rate = pairs[:, 0:LANES], pairs[:, LANES:]
    inverse = lax.rsqrt(square)
    radius = square * inverse
    inverse2 = inverse * inverse
    near = jnp.clip(OUTER_RADIUS / SPAN - radius * (1.0 / SPAN), 0.0, 1.0)
    weight = (near * near) * (3.0 - 2.0 * near) * (inverse * inverse2)
    turned = weight * (rate * inverse2)
    weight_h = weight.astype(BF16)
    weight_l = (weight - weight_h.astype(F32)).astype(BF16)
    turned_h = turned.astype(BF16)
    turned_l = (turned - turned_h.astype(F32)).astype(BF16)
    matrix = jnp.concatenate(
        [
            jnp.concatenate([weight_h, turned_h], axis=1),
            jnp.concatenate([weight_l, turned_l], axis=1),
        ],
        axis=0,
    )
    values = jnp.concatenate([position, velocity, one, nought], axis=0) * mass
    values = jnp.concatenate([*three(values), zeros8], axis=0).astype(BF16)
    sums = jnp.dot(jnp.concatenate([values, values], axis=1), matrix, preferred_element_type=F32)
    sums = sums[0:8] + sums[8:16] + sums[16:24]
    plain, bent = sums[:, 0:LANES], sums[:, LANES:]
    acceleration = plain[0:3] - position * plain[6:7]
    jerk = plain[3:6] - velocity * plain[6:7] - 3.0 * (bent[0:3] - position * bent[6:7])
    return acceleration, jerk


def far_field(pos_ref, every_ref, far_ref):
    stars = pos_ref.shape[1]
    domains = every_ref.shape[0]
    group = min(32, domains)

    def chunk(number, carry):
        columns = pl.ds(pl.multiple_of(number * LANES, LANES), LANES)
        star = [jnp.broadcast_to(pos_ref[axis : axis + 1, columns], (CELLS, LANES)) for axis in range(3)]

        def some(step, total):
            rows = every_ref[pl.ds(pl.multiple_of(step * group, group), group), :]
            table = rows.T
            for k in range(group):
                mass, *centre = [
                    jnp.broadcast_to(table[c * CELLS : (c + 1) * CELLS, k : k + 1], (CELLS, LANES))
                    for c in range(4)
                ]
                offset = [c - s for c, s in zip(centre, star)]
                square = offset[0] * offset[0] + offset[1] * offset[1] + offset[2] * offset[2] + SOFTENING
                inverse = lax.rsqrt(square)
                fraction = jnp.clip(square * inverse * (1.0 / SPAN) - INNER_RADIUS / SPAN, 0.0, 1.0)
                weight = mass * (fraction * fraction * (3.0 - 2.0 * fraction)) * (inverse * inverse * inverse)
                total = tuple(t + weight * o for t, o in zip(total, offset))
            return total

        total = lax.fori_loop(
            0, domains // group, some, tuple(jnp.zeros((CELLS, LANES), F32) for _ in range(3))
        )
        far_ref[:, columns] = jnp.concatenate([jnp.sum(t, axis=0, keepdims=True) for t in total], axis=0)
        return carry

    lax.fori_loop(0, stars // LANES, chunk, 0)


TOGETHER = 2


def step_stars(
    capacity, lanes, steps_ref, owner_ref, pos_ref, rows_ref, near_ref, every_ref, index_ref,
    far_ref, out_ref, member_ref, slot_ref, order_ref, tally_ref,
):
    blocks, length = index_ref.shape
    far_field(pos_ref, every_ref, far_ref)
    out_ref[...] = jnp.zeros_like(out_ref)

    def clear(i, carry):
        tally_ref[i] = 0
        return carry

    lax.fori_loop(0, tally_ref.shape[0], clear, 0)
    base = SUBMAX + 2

    def count(b, carry):
        n = steps_ref[b]
        tally_ref[n + 1] = tally_ref[n + 1] + 1
        owner = owner_ref[b, 0]
        rank = tally_ref[base + owner]
        tally_ref[base + owner] = rank + 1
        slot_ref[b] = owner * capacity + rank
        return carry

    lax.fori_loop(0, blocks, count, 0)

    def sum_up(i, carry):
        tally_ref[i] = tally_ref[i] + tally_ref[i - 1]
        return carry

    lax.fori_loop(1, base, sum_up, 0)

    def place(b, carry):
        n = steps_ref[b]
        at = tally_ref[n]
        order_ref[at] = b
        tally_ref[n] = at + 1
        return carry

    lax.fori_loop(0, blocks, place, 0)

    own_chunks = rows_ref.shape[0]
    per = near_ref.shape[1]
    group = 8
    for first in range(0, blocks, group):
        indices = [jnp.broadcast_to(index_ref[b : b + 1, :], (8, LANES)) for b in range(first, first + group)]
        lane = [i & (LANES - 1) for i in indices]
        chunk = [i >> 7 for i in indices]

        def found(piece, number, carry):
            return tuple(
                jnp.where(c == number, jnp.take_along_axis(piece, l, axis=1), old)
                for c, l, old in zip(chunk, lane, carry)
            )

        carry = tuple(jnp.zeros((8, LANES), F32) for _ in range(group))
        for number in range(own_chunks):
            carry = found(rows_ref[number], number, carry)

        def around(number, carry):
            for part in range(per):
                carry = found(near_ref[number, part], own_chunks + number * per + part, carry)
            return carry

        carry = lax.fori_loop(0, near_ref.shape[0], around, carry)
        for b, value in enumerate(carry):
            member_ref[first + b] = value

    def bunch(number, carry):
        names = [order_ref[number * TOGETHER + g] for g in range(TOGETHER)]
        counts = [steps_ref[name] for name in names]
        most = counts[-1]
        data = []
        state = []
        for name, n in zip(names, counts):
            value = member_ref[name]
            middle = jnp.sum(value[0:6], axis=1, keepdims=True) * (1.0 / length)
            moved = value[0:6] - middle
            mass = value[6:7]
            steps = jnp.full((3, LANES), n, jnp.int32)
            width = TIME_STEP / jnp.maximum(steps.astype(F32), 1.0)
            drift = jnp.broadcast_to(middle[3:6], (3, LANES)) * TIME_STEP
            data.append((mass, steps, width, drift, moved))
            position, velocity = moved[0:3], moved[3:6]
            state.append((position, velocity, *forces(position, velocity, mass)))

        def advance(step, state):
            after = []
            for (mass, steps, width, drift, moved), (position, velocity, acc, jerk) in zip(data, state):
                squared = width * width
                predicted = (
                    position + width * velocity + 0.5 * squared * acc + squared * width * (1.0 / 6.0) * jerk
                )
                predicted_vel = velocity + width * acc + 0.5 * squared * jerk
                acc_new, jerk_new = forces(predicted, predicted_vel, mass)
                velocity_new = (
                    velocity + 0.5 * width * (acc + acc_new) + squared * (1.0 / 12.0) * (jerk - jerk_new)
                )
                position_new = (
                    position + 0.5 * width * (velocity + velocity_new) + squared * (1.0 / 12.0) * (acc - acc_new)
                )
                live = steps > step
                after.append(
                    tuple(
                        jnp.where(live, new, old)
                        for new, old in (
                            (position_new, position), (velocity_new, velocity), (acc_new, acc), (jerk_new, jerk),
                        )
                    )
                )
            return tuple(after)

        state = lax.fori_loop(0, most, advance, tuple(state))
        for name, (mass, steps, width, drift, moved), (position, velocity, acc, jerk) in zip(names, data, state):
            change = jnp.concatenate([position - moved[0:3] + drift, velocity - moved[3:6]], axis=0)
            at = pl.multiple_of(slot_ref[name] * length, length)
            out_ref[:, pl.ds(at, length)] = change
        return carry

    lax.fori_loop(0, blocks // TOGETHER, bunch, 0)


def deliver(lanes, packed_ref, out_ref, own_sem, sems):
    here = tuple(lax.axis_index(axis) for axis in AXES)
    me = here[2]
    part = packed_ref.shape[1] // lanes
    barrier = pltpu.get_barrier_semaphore()

    def columns(number):
        return pl.ds(pl.multiple_of(number * part, LANES), part)

    own = pltpu.make_async_copy(packed_ref.at[:, columns(me)], out_ref.at[:, columns(me)], own_sem)
    own.start()

    def other(step):
        there = lax.rem(me + step, lanes)
        return there, (here[0], here[1], there)

    def greet(step, carry):
        pl.semaphore_signal(barrier, inc=1, device_id=other(step)[1], device_id_type=MESH)
        return carry

    lax.fori_loop(1, lanes, greet, 0)
    pl.semaphore_wait(barrier, lanes - 1)

    def send(step, carry):
        there, device = other(step)
        pltpu.make_async_remote_copy(
            src_ref=packed_ref.at[:, columns(there)],
            dst_ref=out_ref.at[:, columns(me)],
            send_sem=sems.at[0],
            recv_sem=sems.at[1],
            device_id=device,
            device_id_type=MESH,
        ).start()
        return carry

    lax.fori_loop(1, lanes, send, 0)
    own.wait()
    rest = packed_ref.at[:, pl.ds(0, (lanes - 1) * part)]
    pltpu.make_async_copy(rest, rest, sems.at[0]).wait()
    pltpu.make_async_copy(rest, rest, sems.at[1]).wait()


def vmem(count):
    return [pl.BlockSpec(memory_space=pltpu.VMEM)] * count


def on_device(
    sizes, positions, velocities, star_mass, far_previous, cell_index, ghost_list, block_index, block_owner, substeps
):
    lanes = sizes[2]
    domains = sizes[0] * sizes[1] * sizes[2]
    blocks, length = block_index.shape
    capacity = max(2, 2 * BLOCKS_DEV // lanes)
    stars, ghosts = positions.shape[1], ghost_list.shape[0]
    shape = jax.ShapeDtypeStruct
    rows, sent, moment = pl.pallas_call(
        prepare,
        out_shape=(
            shape((stars // LANES, 8, LANES), F32),
            shape((ghosts // LANES, 8, LANES), F32),
            shape((1, 1, LANES), F32),
        ),
        in_specs=vmem(6),
        out_specs=tuple(vmem(3)),
        name="prepare",
    )(
        positions,
        velocities,
        star_mass.reshape(1, stars),
        far_previous,
        cell_index.reshape(1, stars),
        ghost_list.reshape(1, ghosts),
    )
    near, every = pl.pallas_call(
        functools.partial(exchange, sizes),
        out_shape=(shape((27, *sent.shape), F32), shape((domains, 1, LANES), F32)),
        in_specs=vmem(2),
        out_specs=tuple(vmem(2)),
        scratch_shapes=[
            pltpu.SemaphoreType.DMA,
            pltpu.SemaphoreType.DMA((2,)),
            pltpu.SemaphoreType.DMA((27,)),
            pltpu.SemaphoreType.DMA((27,)),
        ],
        compiler_params=pltpu.CompilerParams(collective_id=0, has_side_effects=True),
        name="exchange",
    )(sent, moment)
    smem = pl.BlockSpec(memory_space=pltpu.SMEM)
    far_acc, packed = pl.pallas_call(
        functools.partial(step_stars, capacity, lanes),
        out_shape=(shape((3, stars), F32), shape((6, lanes * capacity * length), F32)),
        in_specs=[smem, smem, *vmem(5)],
        out_specs=tuple(vmem(2)),
        scratch_shapes=[
            pltpu.VMEM((blocks, 8, LANES), F32),
            pltpu.SMEM((blocks,), jnp.int32),
            pltpu.SMEM((blocks,), jnp.int32),
            pltpu.SMEM((SUBMAX + 2 + lanes,), jnp.int32),
        ],
        name="step_stars",
    )(substeps, block_owner, positions, rows, near, every.reshape(domains, LANES), block_index)
    arrived = pl.pallas_call(
        functools.partial(deliver, lanes),
        out_shape=shape(packed.shape, F32),
        in_specs=vmem(1),
        out_specs=vmem(1)[0],
        scratch_shapes=[pltpu.SemaphoreType.DMA, pltpu.SemaphoreType.DMA((2,))],
        compiler_params=pltpu.CompilerParams(collective_id=1, has_side_effects=True),
        name="deliver",
    )(packed)
    return far_acc, arrived


def solution(mesh):
    split = P(AXES)
    wide = P(None, AXES)
    tall = P(AXES, None)
    return jax.shard_map(
        functools.partial(on_device, tuple(mesh.shape[axis] for axis in AXES)),
        mesh=mesh,
        in_specs=(wide, wide, split, wide, split, split, tall, tall, split),
        out_specs=(wide, wide),
        check_vma=False,
    )
```

time: 183 us -> 56 us (0.31)
  blocking collectives: 70.8 us -> 0 us
  other arithmetic: 70.5 us -> 0 us
  Pallas kernels: 0 us -> 51.9 us
  starting transfers between devices: 12.2 us -> 0 us
  waiting for transfers between devices: 12.2 us -> 0 us
  local copies, waits for them, and re-layouts: 13.2 us -> 2.89 us
  matrix products: 1.99 us -> 0 us
    all_gather x1 -> x0, blocking collectives: 70.8 us -> none  [on_device(): lax.all_gather(moments, ('gx', 'gy', 'gz'), axis=1, tiled=True)]
    reduce_sum x75 -> x0, other arithmetic: 53.8 us -> none  [the longest x36 34.4 us: evaluate(): acceleration = jnp.sum(weight[None] * offset, axis=-1)]
    pallas_call x0 -> x4, Pallas kernels: none -> 51.9 us  [the longest x1 32.9 us: on_device(): pl.pallas_call(functools.partial(step_stars, capacity, lanes), out_shape=...]
    ppermute x6 -> x0, waiting for transfers between devices: 8.9 us -> none  [the longest x3 8.46 us: padded(): lax.ppermute(head, axis, [((i + 1) % count, i) for i in range(ends)])]
    ppermute x6 -> x0, starting transfers between devices: 8.86 us -> none  [the longest x3 4.99 us: padded(): lax.ppermute(tail, axis, [(i, (i + 1) % count) for i in range(ends)])]
    gather x3 -> x0, local copies, waits for them, and re-layouts: 8.6 us -> none  [the longest x2 7.87 us: on_device(): gathered = pool[:, block_index]]
    mul x40 -> x0, other arithmetic: 7.44 us -> none  [the longest x36 7.41 us: evaluate(): 3.0 * radial_rate[None] * offset]
    add x62 -> x0, other arithmetic: 5.59 us -> none  [the longest x32 2.55 us: integrate(): predicted_vel = velocity + widths * acc_old + 0.5 * squared * jerk_old]
  transfers between devices with their start and end apart: 7 -> 0, of which waited for: 4 -> 0; matrix products, arithmetic and copies ran while one was open for 3% -> 0% of each run, Pallas kernels for 0% -> 0%
where the time goes in v1:
time: 56 us; the launch traced here: 55.4 us
  Pallas kernels  51.9 us (93%)
  local copies, waits for them, and re-layouts  2.89 us (5%)
  between operations  0.66 us (1%)
    pallas_call x1, Pallas kernels, on_device(): pl.pallas_call(functools.partial(step_stars, capacity, lanes), out_shape=...  32.9 us
    pallas_call x1, Pallas kernels, on_device(): pl.pallas_call(functools.partial(exchange, sizes), out_shape=(shape((27,...  11.6 us
    pallas_call x1, Pallas kernels, on_device(): pl.pallas_call(functools.partial(deliver, lanes), out_shape=shape(packed....  5.89 us
    unnamed x4, local copies, waits for them, and re-layouts  2.89 us
    pallas_call x1, Pallas kernels, on_device(): pl.pallas_call(prepare, out_shape=(shape((stars // LANES, 8, LANES), F32)...  1.51 us

profile of v1, /device:TPU:0, one launch (start us, length us, event | category | flops | bytes accessed | tf_op | source)
XLA Modules:
  0.0 55.4 jit_solution(8092769754381849059)
XLA Ops:
  0.6 0.0 copy-start
  0.6 0.6 %copy-done = s32[16,1]{0,1:T(1,128)S(1)} copy-done((s32[16,1]{0,1:T(1,128)S(1)}, s32[16,1]{0,1:T(1,128)}, u32[]{:S(2)}) %copy-start) | copy-done | bytes 88
  1.3 0.7 %copy.11.owner_ref = s32[16,1]{1,0:T(8,128)} copy(s32[16,1]{0,1:T(1,128)S(1)} %copy-done) | data formatting | bytes 128 | tf_op args[7]
  2.0 1.5 %prepare.1 = (f32[4,8,128]{2,1,0:T(8,128)}, f32[2,8,128]{2,1,0:T(8,128)}, f32[1,1,128]{2,1,0:T(1,128)}) custom-call(f32[3,512]{1,0:T(4,128)} %pos_ref.3, f32[3,512]{1,0:T(4,128)} %vel_ref.1, f32[1,512]{1,0:T(1,128)} %bitcast.5, f32[3,512]{1,0:T(4,128)} %far_ref.1, s32[1,512]{1,0:T(1,128)} %bitcast.6, s32[1,256]{1,0:T(1,128)} %bitcast.7), custom_call_target="tpu_custom_call" | custom-call | tf_op jit(solution)/shard_map/prepare/pallas_call | solution.py:428
  3.5 11.6 %exchange.1 = (f32[27,2,8,128]{3,2,1,0:T(8,128)}, f32[32,1,128]{2,1,0:T(1,128)}) custom-call(f32[2,8,128]{2,1,0:T(8,128)} %get-tuple-element.10.sent_ref, f32[1,1,128]{2,1,0:T(1,128)} %get-tuple-element.11.moment_ref), custom_call_target="tpu_custom_call" | custom-call | tf_op jit(solution)/shard_map/exchange/pallas_call | solution.py:446
  15.1 32.9 %step_stars.1 = (f32[3,512]{1,0:T(4,128)}, f32[6,4096]{1,0:T(8,128)}) custom-call(s32[16]{0:T(128)} %steps_ref.1, s32[16,1]{1,0:T(8,128)} %copy.11.owner_ref, f32[3,512]{1,0:T(4,128)} %pos_ref.3, f32[4,8,128]{2,1,0:T(8,128)} %get-tuple-element.9.rows_ref, f32[27,2,8,128]{3,2,1,0:T(8,128)} %get-tuple-element.12.near_ref, f32[32,128]{1,0:T(8,128)} %bitcast.4, ...), custom_call_target="tpu_custom_call" | custom-call | tf_op jit(solution)/shard_map/step_stars/pallas_call | solution.py:461
  48.0 5.9 %deliver.1 = f32[6,4096]{1,0:T(8,128)} custom-call(f32[6,4096]{1,0:T(8,128)} %get-tuple-element.15.packed_ref), custom_call_target="tpu_custom_call" | custom-call | tf_op jit(solution)/shard_map/deliver/pallas_call | solution.py:474
  53.9 1.6 %copy.13 = f32[6,4096]{1,0:T(8,128)} copy(f32[6,4096]{1,0:T(8,128)} %deliver.1) | data formatting | bytes 196608
Async XLA Ops:
  0.6 0.7 %copy-start = (s32[16,1]{0,1:T(1,128)S(1)}, s32[16,1]{0,1:T(1,128)}, u32[]{:S(2)}) copy-start(s32[16,1]{0,1:T(1,128)} %param.16) | copy-start | bytes 196

commit v2 on v1

--- a/solution.py
+++ b/solution.py
@@ -245,76 +245,64 @@
     lax.fori_loop(0, stars // LANES, chunk, 0)
 
 
-TOGETHER = 2
+TOGETHER = 8
 
 
 def step_stars(
-    capacity, lanes, steps_ref, owner_ref, pos_ref, rows_ref, near_ref, every_ref, index_ref,
-    far_ref, out_ref, member_ref, slot_ref, order_ref, tally_ref,
+    sizes, capacity, steps_ref, owner_ref, rows_ref, near_ref, index_ref, out_ref, member_ref, slot_ref, order_ref,
 ):
     blocks, length = index_ref.shape
-    far_field(pos_ref, every_ref, far_ref)
     out_ref[...] = jnp.zeros_like(out_ref)
 
-    def clear(i, carry):
-        tally_ref[i] = 0
-        return carry
-
-    lax.fori_loop(0, tally_ref.shape[0], clear, 0)
-    base = SUBMAX + 2
-
-    def count(b, carry):
-        n = steps_ref[b]
-        tally_ref[n + 1] = tally_ref[n + 1] + 1
-        owner = owner_ref[b, 0]
-        rank = tally_ref[base + owner]
-        tally_ref[base + owner] = rank + 1
-        slot_ref[b] = owner * capacity + rank
-        return carry
-
-    lax.fori_loop(0, blocks, count, 0)
-
-    def sum_up(i, carry):
-        tally_ref[i] = tally_ref[i] + tally_ref[i - 1]
-        return carry
-
-    lax.fori_loop(1, base, sum_up, 0)
-
-    def place(b, carry):
-        n = steps_ref[b]
-        at = tally_ref[n]
-        order_ref[at] = b
-        tally_ref[n] = at + 1
-        return carry
-
-    lax.fori_loop(0, blocks, place, 0)
+    counts = [steps_ref[b] for b in range(blocks)]
+    owners = [owner_ref[b] for b in range(blocks)]
+    places = [jnp.int32(0)] * blocks
+    for b in range(blocks):
+        rank = jnp.int32(0)
+        for earlier in range(b):
+            before = (counts[earlier] <= counts[b]).astype(jnp.int32)
+            places[b] = places[b] + before
+            places[earlier] = places[earlier] + (1 - before)
+            rank = rank + (owners[earlier] == owners[b]).astype(jnp.int32)
+        slot_ref[b] = owners[b] * capacity + rank
+    for b in range(blocks):
+        order_ref[places[b]] = b
 
     own_chunks = rows_ref.shape[0]
     per = near_ref.shape[1]
-    group = 8
-    for first in range(0, blocks, group):
-        indices = [jnp.broadcast_to(index_ref[b : b + 1, :], (8, LANES)) for b in range(first, first + group)]
-        lane = [i & (LANES - 1) for i in indices]
-        chunk = [i >> 7 for i in indices]
-
-        def found(piece, number, carry):
-            return tuple(
-                jnp.where(c == number, jnp.take_along_axis(piece, l, axis=1), old)
-                for c, l, old in zip(chunk, lane, carry)
-            )
-
-        carry = tuple(jnp.zeros((8, LANES), F32) for _ in range(group))
-        for number in range(own_chunks):
-            carry = found(rows_ref[number], number, carry)
-
-        def around(number, carry):
-            for part in range(per):
-                carry = found(near_ref[number, part], own_chunks + number * per + part, carry)
-            return carry
-
-        carry = lax.fori_loop(0, near_ref.shape[0], around, carry)
-        for b, value in enumerate(carry):
-            member_ref[first + b] = value
+    indices = [jnp.broadcast_to(index_ref[b : b + 1, :], (8, LANES)) for b in range(blocks)]
+    lane = [i & (LANES - 1) for i in indices]
+    chunk = [i >> 7 for i in indices]
+
+    def found(piece, number, carry):
+        return tuple(
+            jnp.where(c == number, jnp.take_along_axis(piece, l, axis=1), old)
+            for c, l, old in zip(chunk, lane, carry)
+        )
+
+    carry = tuple(jnp.zeros((8, LANES), F32) for _ in range(blocks))
+    for number in range(own_chunks):
+        carry = found(rows_ref[number], number, carry)
+    def reach(slot, carry):
+        for part in range(per):
+            carry = found(near_ref[slot, part], own_chunks + slot * per + part, carry)
+        return carry
+
+    bounds = []
+    for axis, size in zip(AXES, sizes):
+        at = lax.axis_index(axis)
+        bounds.append((jnp.where(at > 0, 0, 1), jnp.where(at < size - 1, 3, 2)))
+    (low_x, high_x), (low_y, high_y), (low_z, high_z) = bounds
+    wide_y, wide_z = high_y - low_y, high_z - low_z
+
+    def visit(step, carry):
+        number = (low_x + step // (wide_y * wide_z)) * 9
+        number = number + (low_y + step // wide_z % wide_y) * 3 + low_z + step % wide_z
+        return reach(number, carry)
+
+    carry = lax.fori_loop(0, (high_x - low_x) * wide_y * wide_z, visit, carry)
+    for b, value in enumerate(carry):
+        member_ref[b] = value
 
     def bunch(number, carry):
         names = [order_ref[number * TOGETHER + g] for g in range(TOGETHER)]
@@ -370,7 +358,7 @@
     lax.fori_loop(0, blocks // TOGETHER, bunch, 0)
 
 
-def deliver(lanes, packed_ref, out_ref, own_sem, sems):
+def deliver(lanes, packed_ref, pos_ref, every_ref, out_ref, far_ref, own_sem, sems):
     here = tuple(lax.axis_index(axis) for axis in AXES)
     me = here[2]
     part = packed_ref.shape[1] // lanes
@@ -406,6 +394,7 @@
         return carry
 
     lax.fori_loop(1, lanes, send, 0)
+    far_field(pos_ref, every_ref, far_ref)
     own.wait()
     rest = packed_ref.at[:, pl.ds(0, (lanes - 1) * part)]
     pltpu.make_async_copy(rest, rest, sems.at[0]).wait()
@@ -458,28 +447,27 @@
         name="exchange",
     )(sent, moment)
     smem = pl.BlockSpec(memory_space=pltpu.SMEM)
-    far_acc, packed = pl.pallas_call(
-        functools.partial(step_stars, capacity, lanes),
-        out_shape=(shape((3, stars), F32), shape((6, lanes * capacity * length), F32)),
-        in_specs=[smem, smem, *vmem(5)],
-        out_specs=tuple(vmem(2)),
+    packed = pl.pallas_call(
+        functools.partial(step_stars, sizes, capacity),
+        out_shape=shape((6, lanes * capacity * length), F32),
+        in_specs=[smem, smem, *vmem(3)],
+        out_specs=vmem(1)[0],
         scratch_shapes=[
             pltpu.VMEM((blocks, 8, LANES), F32),
             pltpu.SMEM((blocks,), jnp.int32),
             pltpu.SMEM((blocks,), jnp.int32),
-            pltpu.SMEM((SUBMAX + 2 + lanes,), jnp.int32),
         ],
         name="step_stars",
-    )(substeps, block_owner, positions, rows, near, every.reshape(domains, LANES), block_index)
-    arrived = pl.pallas_call(
+    )(substeps, block_owner.reshape(blocks), rows, near, block_index)
+    arrived, far_acc = pl.pallas_call(
         functools.partial(deliver, lanes),
-        out_shape=shape(packed.shape, F32),
-        in_specs=vmem(1),
-        out_specs=vmem(1)[0],
+        out_shape=(shape(packed.shape, F32), shape((3, stars), F32)),
+        in_specs=vmem(3),
+        out_specs=tuple(vmem(2)),
         scratch_shapes=[pltpu.SemaphoreType.DMA, pltpu.SemaphoreType.DMA((2,))],
         compiler_params=pltpu.CompilerParams(collective_id=1, has_side_effects=True),
         name="deliver",
-    )(packed)
+    )(packed, positions, every.reshape(domains, LANES))
     return far_acc, arrived
 
 

time: 56 us -> 38.3 us (0.68)
  Pallas kernels: 51.9 us -> 34.1 us
    pallas_call x2, Pallas kernels: 38.8 us -> 21 us  [the longest x1 14 us: on_device(): pl.pallas_call(functools.partial(step_stars, sizes, capacity), out_shape=...]
    unnamed x4 -> x2, local copies, waits for them, and re-layouts: 2.89 us -> 2.86 us
where the time goes in v2:
time: 38.3 us; the launch traced here: 37.6 us
  Pallas kernels  34.1 us (89%)
  local copies, waits for them, and re-layouts  2.86 us (7%)
  between operations  0.65 us (2%)
    pallas_call x1, Pallas kernels, on_device(): pl.pallas_call(functools.partial(step_stars, sizes, capacity), out_shape=...  14 us
    pallas_call x1, Pallas kernels, on_device(): pl.pallas_call(functools.partial(exchange, sizes), out_shape=(shape((27,...  11.6 us
    pallas_call x1, Pallas kernels, on_device(): pl.pallas_call(functools.partial(deliver, lanes), out_shape=(shape(packed...  6.98 us
    unnamed x2, local copies, waits for them, and re-layouts  2.86 us
    pallas_call x1, Pallas kernels, on_device(): pl.pallas_call(prepare, out_shape=(shape((stars // LANES, 8, LANES), F32)...  1.52 us

profile of v2, /device:TPU:0, one launch (start us, length us, event | category | flops | bytes accessed | tf_op | source)
XLA Modules:
  0.0 37.6 jit_solution(16784290074008243376)
XLA Ops:
  0.6 1.5 %prepare.1 = (f32[4,8,128]{2,1,0:T(8,128)}, f32[2,8,128]{2,1,0:T(8,128)}, f32[1,1,128]{2,1,0:T(1,128)}) custom-call(f32[3,512]{1,0:T(4,128)} %pos_ref.3, f32[3,512]{1,0:T(4,128)} %vel_ref.1, f32[1,512]{1,0:T(1,128)} %bitcast.6, f32[3,512]{1,0:T(4,128)} %far_ref.1, s32[1,512]{1,0:T(1,128)} %bitcast.7, s32[1,256]{1,0:T(1,128)} %bitcast.8), custom_call_target="tpu_custom_call" | custom-call | tf_op jit(solution)/shard_map/prepare/pallas_call | solution.py:417
  2.1 11.6 %exchange.1 = (f32[27,2,8,128]{3,2,1,0:T(8,128)}, f32[32,1,128]{2,1,0:T(1,128)}) custom-call(f32[2,8,128]{2,1,0:T(8,128)} %get-tuple-element.10.sent_ref, f32[1,1,128]{2,1,0:T(1,128)} %get-tuple-element.11.moment_ref), custom_call_target="tpu_custom_call" | custom-call | tf_op jit(solution)/shard_map/exchange/pallas_call | solution.py:435
  13.7 14.0 %step_stars.1.packed_ref = f32[6,4096]{1,0:T(8,128)} custom-call(s32[16]{0:T(128)} %steps_ref.1, s32[16]{0:T(128)} %bitcast.9, f32[4,8,128]{2,1,0:T(8,128)} %get-tuple-element.9.rows_ref, f32[27,2,8,128]{3,2,1,0:T(8,128)} %get-tuple-element.12.near_ref, s32[16,128]{1,0:T(8,128)} %index_ref.1), custom_call_target="tpu_custom_call" | custom-call | tf_op jit(solution)/shard_map/step_stars/pallas_call | solution.py:450
  27.7 7.0 %deliver.1 = (f32[6,4096]{1,0:T(8,128)}, f32[3,512]{1,0:T(4,128)}) custom-call(f32[6,4096]{1,0:T(8,128)} %step_stars.1.packed_ref, f32[3,512]{1,0:T(4,128)} %pos_ref.3, f32[32,128]{1,0:T(8,128)} %bitcast.5), custom_call_target="tpu_custom_call" | custom-call | tf_op jit(solution)/shard_map/deliver/pallas_call | solution.py:462
  34.7 1.3 %copy.13 = f32[3,512]{1,0:T(4,128)} copy(f32[3,512]{1,0:T(4,128)} %get-tuple-element.18) | data formatting | bytes 12288
  36.0 1.6 %copy.14 = f32[6,4096]{1,0:T(8,128)} copy(f32[6,4096]{1,0:T(8,128)} %get-tuple-element.19) | data formatting | bytes 196608

commit v3 on v2

--- a/solution.py
+++ b/solution.py
@@ -72,7 +72,10 @@
     return number // (sizes[1] * sizes[2]), number // sizes[2] % sizes[1], number % sizes[2]
 
 
-def exchange(sizes, sent_ref, moment_ref, near_ref, every_ref, own_sem, moment_sems, send_sems, recv_sems):
+def exchange(
+    sizes, pos_ref, vel_ref, mass_ref, far_ref, cell_ref, ghost_ref, rows_ref, near_ref, every_ref,
+    sent_ref, moment_ref, own_sem, moment_sems, send_sems, recv_sems,
+):
     count = sizes[0] * sizes[1] * sizes[2]
     here = tuple(lax.axis_index(axis) for axis in AXES)
     me = (here[0] * sizes[1] + here[1]) * sizes[2] + here[2]
@@ -86,6 +89,7 @@
         return carry
 
     lax.fori_loop(1, count, greet, 0)
+    prepare(pos_ref, vel_ref, mass_ref, far_ref, cell_ref, ghost_ref, rows_ref, sent_ref, moment_ref)
     own = pltpu.make_async_copy(moment_ref.at[0], every_ref.at[0], own_sem)
     own.start()
     pl.semaphore_wait(barrier, count - 1)
@@ -146,37 +150,28 @@
 def forces(position, velocity, mass):
     norm = jnp.sum(position * position, axis=0, keepdims=True) + 0.5 * SOFTENING
     mixed = jnp.sum(position * velocity, axis=0, keepdims=True)
-    one = jnp.ones_like(norm)
-    nought = jnp.zeros_like(norm)
-    nought3 = jnp.zeros_like(position)
+    nought = jnp.zeros((2, LANES), F32)
+    row = lax.broadcasted_iota(jnp.int32, (8, LANES), 0)
+    state_row, norm_row, mixed_row = row < 6, row == 6, row == 7
+    norm_one, mixed_one = jnp.where(norm_row, 1.0, 0.0), jnp.where(mixed_row, 1.0, 0.0)
+    scale = jnp.where(row < 3, -2.0, 0.0)
     left = jnp.concatenate([position, velocity, norm, mixed], axis=0)
-    left_h, left_m, left_l = three(left)
-    ones8 = jnp.ones_like(left)
-    zeros8 = jnp.zeros_like(left)
-    left_all = jnp.concatenate([left_h, left_h, left_h, left_m, left_m, left_l, ones8, zeros8], axis=0)
-
-    pos_parts = three(position)
-    vel_parts = three(velocity)
-    norm_parts = three(norm)
-    mixed_parts = three(mixed)
-
-    def right(kind):
-        if kind == 0:
-            groups = [
-                jnp.concatenate([-2.0 * part, nought3, one if k == 0 else nought, nought], axis=0)
-                for k, part in enumerate(pos_parts)
-            ]
-            last = jnp.concatenate([*norm_parts, nought3, nought, nought], axis=0)
-        else:
-            groups = [
-                jnp.concatenate([-v, -p, nought, one if k == 0 else nought], axis=0)
-                for k, (p, v) in enumerate(zip(pos_parts, vel_parts))
-            ]
-            last = jnp.concatenate([*mixed_parts, nought3, nought, nought], axis=0)
-        first, second, third = groups
-        return jnp.concatenate([first, second, third, first, second, first, last, zeros8], axis=0)
-
-    right_all = jnp.concatenate([right(0), right(1)], axis=1)
+    high, middle, low = three(left)
+    high_one, middle_one = jnp.where(state_row, high, 1.0), jnp.where(state_row, middle, 1.0)
+    left_all = jnp.concatenate([high, high_one, high_one, middle, middle_one, low], axis=0)
+    turn = three(jnp.concatenate([-velocity, -position, nought], axis=0))
+
+    def right(parts, mine, one):
+        first = jnp.where(mine, one, parts[0])
+        second = jnp.where(mine, high, parts[1])
+        third = jnp.where(mine, middle, parts[2])
+        fourth = jnp.where(mine, low, parts[1])
+        return jnp.concatenate([first, second, third, first, fourth, first], axis=0)
+
+    right_all = jnp.concatenate(
+        [right((high * scale, middle * scale, low * scale), norm_row, norm_one), right(turn, mixed_row, mixed_one)],
+        axis=1,
+    )
     pairs = lax.dot_general(
         left_all.astype(BF16),
         right_all.astype(BF16),
@@ -201,8 +196,8 @@
         ],
         axis=0,
     )
-    values = jnp.concatenate([position, velocity, one, nought], axis=0) * mass
-    values = jnp.concatenate([*three(values), zeros8], axis=0).astype(BF16)
+    values = jnp.where(state_row, left, norm_one) * mass
+    values = jnp.concatenate([*three(values), jnp.zeros_like(values)], axis=0).astype(BF16)
     sums = jnp.dot(jnp.concatenate([values, values], axis=1), matrix, preferred_element_type=F32)
     sums = sums[0:8] + sums[8:16] + sums[16:24]
     plain, bent = sums[:, 0:LANES], sums[:, LANES:]
@@ -401,6 +396,15 @@
     pltpu.make_async_copy(rest, rest, sems.at[1]).wait()
 
 
+def finish(far_ref, arrived_ref, far_out_ref, out_ref, sems):
+    first = pltpu.make_async_copy(arrived_ref, out_ref, sems.at[0])
+    second = pltpu.make_async_copy(far_ref, far_out_ref, sems.at[1])
+    first.start()
+    second.start()
+    first.wait()
+    second.wait()
+
+
 def vmem(count):
     return [pl.BlockSpec(memory_space=pltpu.VMEM)] * count
 
@@ -414,16 +418,26 @@
     capacity = max(2, 2 * BLOCKS_DEV // lanes)
     stars, ghosts = positions.shape[1], ghost_list.shape[0]
     shape = jax.ShapeDtypeStruct
-    rows, sent, moment = pl.pallas_call(
-        prepare,
+    sent = (ghosts // LANES, 8, LANES)
+    rows, near, every = pl.pallas_call(
+        functools.partial(exchange, sizes),
         out_shape=(
             shape((stars // LANES, 8, LANES), F32),
-            shape((ghosts // LANES, 8, LANES), F32),
-            shape((1, 1, LANES), F32),
+            shape((27, *sent), F32),
+            shape((domains, 1, LANES), F32),
         ),
         in_specs=vmem(6),
         out_specs=tuple(vmem(3)),
-        name="prepare",
+        scratch_shapes=[
+            pltpu.VMEM(sent, F32),
+            pltpu.VMEM((1, 1, LANES), F32),
+            pltpu.SemaphoreType.DMA,
+            pltpu.SemaphoreType.DMA((2,)),
+            pltpu.SemaphoreType.DMA((27,)),
+            pltpu.SemaphoreType.DMA((27,)),
+        ],
+        compiler_params=pltpu.CompilerParams(collective_id=0, has_side_effects=True),
+        name="exchange",
     )(
         positions,
         velocities,
@@ -432,20 +446,6 @@
         cell_index.reshape(1, stars),
         ghost_list.reshape(1, ghosts),
     )
-    near, every = pl.pallas_call(
-        functools.partial(exchange, sizes),
-        out_shape=(shape((27, *sent.shape), F32), shape((domains, 1, LANES), F32)),
-        in_specs=vmem(2),
-        out_specs=tuple(vmem(2)),
-        scratch_shapes=[
-            pltpu.SemaphoreType.DMA,
-            pltpu.SemaphoreType.DMA((2,)),
-            pltpu.SemaphoreType.DMA((27,)),
-            pltpu.SemaphoreType.DMA((27,)),
-        ],
-        compiler_params=pltpu.CompilerParams(collective_id=0, has_side_effects=True),
-        name="exchange",
-    )(sent, moment)
     smem = pl.BlockSpec(memory_space=pltpu.SMEM)
     packed = pl.pallas_call(
         functools.partial(step_stars, sizes, capacity),
@@ -468,7 +468,14 @@
         compiler_params=pltpu.CompilerParams(collective_id=1, has_side_effects=True),
         name="deliver",
     )(packed, positions, every.reshape(domains, LANES))
-    return far_acc, arrived
+    return pl.pallas_call(
+        finish,
+        out_shape=(shape(far_acc.shape, F32), shape(arrived.shape, F32)),
+        in_specs=vmem(2),
+        out_specs=(pl.BlockSpec(memory_space=pl.ANY), pl.BlockSpec(memory_space=pl.ANY)),
+        scratch_shapes=[pltpu.SemaphoreType.DMA((2,))],
+        name="finish",
+    )(far_acc, arrived)
 
 
 def solution(mesh):

time: 38.3 us -> 35.5 us (0.927); the launches traced: 37.6 us -> 35.2 us
  local copies, waits for them, and re-layouts: 2.86 us -> 0 us
  Pallas kernels: 34.1 us -> 34.6 us
    unnamed x2 -> x0, local copies, waits for them, and re-layouts: 2.86 us -> none
    pallas_call x1, Pallas kernels: 6.98 us -> 8.18 us  [on_device(): pl.pallas_call(functools.partial(deliver, lanes), out_shape=(shape(packed...]
    pallas_call x1, Pallas kernels: 14 us -> 13.1 us  [on_device(): pl.pallas_call(functools.partial(step_stars, sizes, capacity), out_shape=...]
where the time goes in v3:
time: 35.5 us; the launch traced here: 35.2 us
  Pallas kernels  34.6 us (97%)
  between operations  0.65 us (2%)
    pallas_call x1, Pallas kernels, on_device(): pl.pallas_call(functools.partial(step_stars, sizes, capacity), out_shape=...  13.1 us
    pallas_call x1, Pallas kernels, on_device(): pl.pallas_call(functools.partial(exchange, sizes), out_shape=(shape((star...  11.7 us
    pallas_call x1, Pallas kernels, on_device(): pl.pallas_call(functools.partial(deliver, lanes), out_shape=(shape(packed...  8.18 us
    pallas_call x1, Pallas kernels, on_device(): pl.pallas_call(finish, out_shape=(shape(far_acc.shape, F32), shape(arrive...  1.6 us

profile of v3, /device:TPU:0, one launch (start us, length us, event | category | flops | bytes accessed | tf_op | source)
XLA Modules:
  0.0 35.2 jit_solution(8451219793227054495)
XLA Ops:
  0.6 11.7 %exchange.1 = (f32[4,8,128]{2,1,0:T(8,128)}, f32[27,2,8,128]{3,2,1,0:T(8,128)}, f32[32,1,128]{2,1,0:T(1,128)}) custom-call(f32[3,512]{1,0:T(4,128)} %pos_ref.3, f32[3,512]{1,0:T(4,128)} %vel_ref.1, f32[1,512]{1,0:T(1,128)} %bitcast.6, f32[3,512]{1,0:T(4,128)} %far_ref.1, s32[1,512]{1,0:T(1,128)} %bitcast.7, s32[1,256]{1,0:T(1,128)} %bitcast.8), custom_call_target="tpu_custom_call" | custom-call | tf_op jit(solution)/shard_map/exchange/pallas_call | solution.py:422
  12.3 13.1 %step_stars.1.packed_ref = f32[6,4096]{1,0:T(8,128)} custom-call(s32[16]{0:T(128)} %steps_ref.1, s32[16]{0:T(128)} %bitcast.9, f32[4,8,128]{2,1,0:T(8,128)} %get-tuple-element.7.rows_ref, f32[27,2,8,128]{3,2,1,0:T(8,128)} %get-tuple-element.8.near_ref, s32[16,128]{1,0:T(8,128)} %index_ref.1), custom_call_target="tpu_custom_call" | custom-call | tf_op jit(solution)/shard_map/step_stars/pallas_call | solution.py:450
  25.5 8.2 %deliver.1 = (f32[6,4096]{1,0:T(8,128)}, f32[3,512]{1,0:T(4,128)}) custom-call(f32[6,4096]{1,0:T(8,128)} %step_stars.1.packed_ref, f32[3,512]{1,0:T(4,128)} %pos_ref.3, f32[32,128]{1,0:T(8,128)} %bitcast.5), custom_call_target="tpu_custom_call" | custom-call | tf_op jit(solution)/shard_map/deliver/pallas_call | solution.py:462
  33.6 1.6 %finish.1 = (f32[3,512]{1,0:T(4,128)}, f32[6,4096]{1,0:T(8,128)}) custom-call(f32[3,512]{1,0:T(4,128)} %get-tuple-element.10.far_ref, f32[6,4096]{1,0:T(8,128)} %get-tuple-element.11.arrived_ref), custom_call_target="tpu_custom_call" | custom-call | tf_op jit(solution)/shard_map/finish/pallas_call | solution.py:471
